TPU v7x, 32 devices: a whole 2x2x4 slice. The times are simulated.
32 devices in a mesh: groups: 2 (over x), src: 8 (over z, y), tile: 2 (over core).
Axes of the slice: x: 2, y: 2, z: 4, core: 2. Of those that a mesh axis runs over, the one named last changes fastest.
Arguments:
- mask: float32 [2048, 1024], P(('groups', 'tile')), parts along dimension 0, may hold values from 0 to 1
- target: float32 [2048, 1024], P(('groups', 'tile')), parts along dimension 0, may hold values from 0 to 1
- pupil: float32 [64, 64], replicated, may hold values from 0.1 to 1.9
- source_shift: int32 [24, 2], replicated, may hold values from -24 to 24
- source_weight: float32 [24], replicated, may hold values from 0.25 to 4
Outputs:
- mask_gradient: float32 [2048, 1024], P(('groups', 'tile'), 'src'), parts along dimension 0
There are 2 independent parts, one for each index of `groups`. A program takes and returns all parts, laid end to end along the dimension named above; an argument that names none is the same for every part. Nothing has to cross between parts.
Inputs may be any that keep to these rules, and one draw needn't show every extreme that they name: `source_shift`: integer frequency shifts of the source points.
All inputs are finite; a program needn't handle non-finite values.
Results may differ from a plain program's by a relative error of at most 0.0003.
Values sent between devices are 32-bit elements; how exact they have to be, the bound alone decides.
A program may use at most 128 MiB of HBM per device.

v0:
```python
import numpy as np
import jax
import jax.numpy as jnp
from jax import lax
from jax.sharding import PartitionSpec as P

TS = 512
HALO = 64
PAD = 640
GRID = 128
REACH = 24
exact_mode = lax.Precision.HIGHEST
resist_gain = 25.0
resist_level = 0.25


def tables(freqs, columns):
    pixels = np.arange(PAD)[:, None]
    samples = np.arange(GRID)[None, :] * (PAD // GRID)
    spread = np.ones((PAD, GRID))
    for p in range(1, GRID // 2):
        spread += 2.0 * np.cos(2.0 * np.pi * (p * (pixels - samples) % PAD) / PAD)
    spread /= GRID
    tiles = columns // TS
    across = np.zeros((columns, tiles * GRID))
    for c in range(tiles):
        low, high = (max(0, c * TS - HALO), min(columns, c * TS - HALO + PAD))
        across[low:high, c * GRID : (c + 1) * GRID] = spread[
            low + HALO - c * TS : high + HALO - c * TS
        ]
    bins = np.arange(-freqs // 2 - REACH, freqs // 2 + REACH)[:, None] * np.arange(GRID)[None, :]
    angle = 2.0 * np.pi * (bins % GRID) / GRID
    waves = np.concatenate([np.cos(angle), np.sin(angle)], axis=1)
    return (spread, across, waves)


def rotation(waves, freqs):
    centre = waves[REACH : REACH + freqs]
    cosine, sine = (centre[:, :GRID].T, centre[:, GRID:].T)
    return np.block([[cosine, -sine], [sine, cosine]])


def mm(a, b):
    return jnp.dot(a, b, precision=exact_mode, preferred_element_type=jnp.float32)


def resist_slope(intensity, target):
    printed = jax.nn.sigmoid(resist_gain * (intensity - resist_level))
    return 2.0 * (printed - target) * resist_gain * printed * (1.0 - printed)


def halves(y, tiles, freqs):
    real, imag = ([], [])
    for c in range(tiles):
        top = y[2 * c * freqs : (2 * c + 1) * freqs]
        low = y[(2 * c + 1) * freqs : (2 * c + 2) * freqs]
        real.append(top[:, :GRID] - low[:, GRID:])
        imag.append(top[:, GRID:] + low[:, :GRID])
    return (jnp.concatenate(real, axis=1), jnp.concatenate(imag, axis=1))


def shards(mask, target, pupil, source_shift, source_weight):
    f32 = jnp.float32
    me = lax.axis_index("src")
    n = lax.axis_size("src")
    nt = lax.axis_size("tile")
    own = source_shift.shape[0] // n
    freqs = pupil.shape[0]
    columns = mask.shape[1]
    tiles = columns // TS
    width = columns // n
    spread64, across64, waves64 = tables(freqs, columns)
    spread = jnp.asarray(spread64, f32)
    core = spread[HALO : HALO + TS]
    across = jnp.asarray(across64, f32)
    waves = jnp.asarray(waves64, f32)
    fixed = jnp.asarray(waves64[REACH : REACH + freqs], f32)
    turn = jnp.asarray(rotation(waves64, freqs), f32)
    total = jnp.sum(source_weight)
    scaled = jnp.tile(pupil / (PAD * PAD), (2 * tiles, 1))
    above = lax.ppermute(mask[TS - HALO :], "tile", [(i, i + 1) for i in range(nt - 1)])
    below = lax.ppermute(mask[:HALO], "tile", [(i + 1, i) for i in range(nt - 1)])
    strip = jnp.concatenate([above, mask, below], axis=0)
    low = mm(mm(spread.T, strip), across)
    zc = mm(waves[:, :GRID], low)
    zs = mm(waves[:, GRID:], low)
    fields = []
    light = jnp.zeros((GRID, tiles * GRID), f32)
    for s in range(own):
        a = source_shift[me * own + s, 0] + REACH
        b = source_shift[me * own + s, 1] + REACH
        w = source_weight[me * own + s]
        c_rows = lax.dynamic_slice_in_dim(zc, a, freqs, 0)
        s_rows = lax.dynamic_slice_in_dim(zs, a, freqs, 0)
        shifted = lax.dynamic_slice_in_dim(waves, b, freqs, 0)
        rows = []
        for c in range(tiles):
            cc = c_rows[:, c * GRID : (c + 1) * GRID]
            ss = s_rows[:, c * GRID : (c + 1) * GRID]
            rows.append(jnp.concatenate([cc, -ss], axis=1))
            rows.append(jnp.concatenate([-ss, -cc], axis=1))
        spec = mm(jnp.concatenate(rows, axis=0), shifted.T) * scaled
        real, imag = halves(mm(spec, fixed), tiles, freqs)
        field = mm(turn, jnp.concatenate([real, imag], axis=0))
        fields.append(field)
        light = light + w * (field[:GRID] * field[:GRID] + field[GRID:] * field[GRID:])
    light = lax.psum(light, "src")
    up = mm(core, light)
    backs = []
    for c in range(tiles):
        fine = mm(up[:, c * GRID : (c + 1) * GRID], core.T)
        slope = resist_slope(fine / total, target[:, c * TS : (c + 1) * TS]) / total
        backs.append(mm(slope, core))
    pull = mm(core.T, jnp.concatenate(backs, axis=1))
    pull = jnp.concatenate([pull, pull], axis=0)
    grid_grad = jnp.zeros((GRID, tiles * GRID), f32)
    for s in range(own):
        a = source_shift[me * own + s, 0] + REACH
        b = source_shift[me * own + s, 1] + REACH
        w = source_weight[me * own + s]
        shift_a = lax.dynamic_slice_in_dim(waves, a, freqs, 0)
        shift_b = lax.dynamic_slice_in_dim(waves, b, freqs, 0)
        u = mm(turn.T, fields[s] * pull * (2.0 * w))
        rows = []
        for c in range(tiles):
            re = u[:freqs, c * GRID : (c + 1) * GRID]
            im = u[freqs:, c * GRID : (c + 1) * GRID]
            rows.append(jnp.concatenate([re, im], axis=1))
            rows.append(jnp.concatenate([im, -re], axis=1))
        back = mm(jnp.concatenate(rows, axis=0), fixed.T) * scaled
        real, imag = halves(mm(back, shift_b), tiles, freqs)
        grid_grad = grid_grad + mm(shift_a[:, :GRID].T, real) - mm(shift_a[:, GRID:].T, imag)
    grid_grad = lax.psum(grid_grad, "src")
    cols = lax.dynamic_slice_in_dim(across, me * width, width, 0)
    full = mm(spread, mm(grid_grad, cols.T))
    upper, inner, lower = (full[:HALO], full[HALO : HALO + TS], full[HALO + TS :])
    from_above = lax.ppermute(lower, "tile", [(i, i + 1) for i in range(nt - 1)])
    from_below = lax.ppermute(upper, "tile", [(i + 1, i) for i in range(nt - 1)])
    inner = inner.at[:HALO].add(from_above)
    return inner.at[TS - HALO :].add(from_below)


def solution(mesh):
    placed = (P(("groups", "tile"), None), P(("groups", "tile"), None), P(), P(), P())
    return jax.shard_map(
        shards, mesh=mesh, in_specs=placed, out_specs=P(("groups", "tile"), "src"), check_vma=False
    )
```

profile of v0, /device:TPU:0, one launch (start us, length us, event | category | flops | bytes accessed | tf_op | source)
XLA Modules:
  0.0 207.0 jit_solution(10192906300589848366)
XLA Ops:
  6.6 1.1 fusion.238
  7.7 1.3 collective-permute-start.1
  9.0 3.1 %collective-permute-start = (f32[64,1024]{1,0:T(8,128)S(1)}, f32[64,1024]{1,0:T(8,128)S(1)}, u32[]{:S(2)}, u32[]{:S(2)}) collective-permute-start(f32[64,1024]{1,0:T(8,128)S(1)} %get-tuple-element.29), channel_id=1, source_target_pairs={{0,1},{2,3},{4,5},{6,7},{8,9},{10,11},{12,13},{14,15},{16,17},{18,... | collective-permute-start | bytes 786440 | tf_op jit(solution)/shard_map/ppermute | solution.py:81
  12.0 3.0 %fusion.247 = f32[128,1024]{1,0:T(8,128)S(1)} fusion(f32[512,128]{1,0:T(8,128)} %constant.135, f32[512,1024]{1,0:T(8,128)} %param.14), kind=kOutput, calls=%fused_computation.327 | convolution fusion | flops 805306368 | bytes 2883584 | tf_op jit(solution)/shard_map/dot_general | solution.py:44
  15.1 0.7 constant_dynamic-slice_fusion.4
  23.1 0.7 fusion.246
  23.8 0.6 fusion.248
  24.5 0.7 fusion.10
  25.2 0.6 fusion.249
  26.5 0.4 convolution_multiply_fusion.4
  26.9 0.3 fusion.253
  27.3 0.4 convolution_multiply_fusion.3
  28.1 0.4 convolution_multiply_fusion.5
  28.5 0.3 fusion.252
  28.9 0.4 fusion.161
  29.3 0.4 fusion.168
  29.7 0.4 fusion.154
  30.2 0.4 fusion.12
  30.6 0.4 fusion.11
  31.0 0.4 fusion.13
  31.4 2.4 %fusion.134 = f32[128,256]{0,1:T(8,128)} fusion(f32[256,256]{0,1:T(8,128)S(1)} %fusion.11, f32[256,256]{0,1:T(8,128)S(1)} %fusion.12, f32[256,256]{0,1:T(8,128)S(1)} %fusion.13, f32[]{:T(128)} %bitcast.17, f32[]{:T(128)} %bitcast.9, f32[]{:T(128)} %bitcast.8), kind=kLoop, calls=%fused_computation.152 | loop fusion | flops 458752 | bytes 917516 | tf_op jit(solution)/shard_map/add | solution.py:106
  35.9 0.6 reduce_sum.9
  36.4 70.7 %all-reduce.3.cloned.1.call-done = f32[128,256]{0,1:T(8,128)} async-done(((f32[128,256]{0,1:T(8,128)}), f32[128,256]{0,1:T(8,128)}) %all-reduce.3.cloned.1.call-update) | async-done | bytes 131088 | tf_op jit(solution)/shard_map/psum | solution.py:107
  107.2 1.5 fusion.255
  108.7 1.7 fusion.15
  110.4 1.9 fusion.14
  112.3 1.6 fusion.16
  114.0 1.7 fusion.17
  115.6 1.0 fusion.18
  116.6 0.4 fusion.85
  117.1 0.4 convolution_multiply_fusion
  117.4 0.4 fusion.145
  117.8 0.4 fusion.82
  118.3 0.4 convolution_multiply_fusion.1
  118.6 0.4 fusion.148
  119.0 0.4 fusion.79
  119.5 0.4 convolution_multiply_fusion.2
  119.8 0.4 fusion.151
  120.6 0.4 convolution_subtract_fusion.2
  121.3 0.4 convolution_subtract_fusion.1
  122.0 1.0 convolution_subtract_fusion
  123.1 69.6 %all-reduce.5.cloned.1.call-done = f32[128,256]{1,0:T(8,128)} async-done(((f32[128,256]{1,0:T(8,128)}), f32[128,256]{1,0:T(8,128)}) %all-reduce.5.cloned.1.call-update) | async-done | bytes 131088 | tf_op jit(solution)/shard_map/psum | solution.py:133
  192.7 1.2 fusion.140
  193.9 0.4 fusion.256
  194.4 1.3 collective-permute-start.2
  195.7 1.3 collective-permute-start.3
  197.0 1.8 collective-permute-done.3
  198.8 1.4 fusion.194
  (68 shorter events, 2.5 us)
Async XLA Ops:
  6.5 17.3 %copy-start.12 = (f32[64,128]{1,0:T(8,128)S(1)}, f32[64,128]{1,0:T(8,128)}, u32[]{:S(2)}) copy-start(f32[64,128]{1,0:T(8,128)} %constant.136) | copy-start | bytes 98308
  6.5 8.5 %copy-start.13 = (f32[64,64]{1,0:T(8,128)S(1)}, f32[64,64]{1,0:T(8,128)}, u32[]{:S(2)}) copy-start(f32[64,64]{1,0:T(8,128)} %param.16) | copy-start | bytes 49156
  6.5 8.5 %copy-start.14 = (s32[24,2]{0,1:T(2,128)S(1)}, s32[24,2]{0,1:T(2,128)}, u32[]{:S(2)}) copy-start(s32[24,2]{0,1:T(2,128)} %param.17) | copy-start | bytes 580
  6.5 16.6 %copy-start.15 = (f32[24]{0:T(128)S(1)}, f32[24]{0:T(128)}, u32[]{:S(2)}) copy-start(f32[24]{0:T(128)} %param.18) | copy-start | bytes 292
  6.5 100.6 %all-reduce.3.cloned.1.call-start = ((), (), s32[]{:S(2)}) async-start(), calls=%async_computation | async-start | bytes 262144 | tf_op jit(solution)/shard_map/psum | solution.py:107
  7.7 16.8 %copy-start.11 = (f32[64,128]{1,0:T(8,128)S(1)}, f32[64,128]{1,0:T(8,128)}, u32[]{:S(2)}) copy-start(f32[64,128]{1,0:T(8,128)} %constant.134) | copy-start | bytes 98308
  7.7 16.1 %collective-permute-start.1 = (f32[64,1024]{1,0:T(8,128)S(1)}, f32[64,1024]{1,0:T(8,128)S(1)}, u32[]{:S(2)}, u32[]{:S(2)}) collective-permute-start(f32[64,1024]{1,0:T(8,128)S(1)} %get-tuple-element.30), channel_id=1, source_target_pairs={{1,0},{3,2},{5,4},{7,6},{9,8},{11,10},{13,12},{15,14},{17,16},{19,... | collective-permute-start | bytes 786440 | tf_op jit(solution)/shard_map/ppermute | solution.py:82
  9.0 15.5 %collective-permute-start = (f32[64,1024]{1,0:T(8,128)S(1)}, f32[64,1024]{1,0:T(8,128)S(1)}, u32[]{:S(2)}, u32[]{:S(2)}) collective-permute-start(f32[64,1024]{1,0:T(8,128)S(1)} %get-tuple-element.29), channel_id=1, source_target_pairs={{0,1},{2,3},{4,5},{6,7},{8,9},{10,11},{12,13},{14,15},{16,17},{18,... | collective-permute-start | bytes 786440 | tf_op jit(solution)/shard_map/ppermute | solution.py:81
  15.0 10.1 %copy-start.2 = (f32[1024,256]{1,0:T(8,128)S(1)}, f32[1024,256]{1,0:T(8,128)}, u32[]{:S(2)}) copy-start(f32[1024,256]{1,0:T(8,128)} %constant.130.clone) | copy-start | bytes 3145732
  23.8 2.0 copy-start.10
  24.4 1.7 copy-start.9
  25.1 1.3 copy-start.1
  25.2 1.7 copy-start.6
  27.3 1.6 copy-start.3
  28.0 2.1 %copy-start.5 = (f32[256,64]{1,0:T(8,128)S(1)}, f32[256,64]{1,0:T(8,128)}, u32[]{:S(2)}) copy-start(f32[256,64]{1,0:T(8,128)} %constant.140) | copy-start | bytes 196612
  29.3 77.9 %copy-start = (f32[512,128]{1,0:T(8,128)S(1)}, f32[512,128]{1,0:T(8,128)}, u32[]{:S(2)}) copy-start(f32[512,128]{1,0:T(8,128)} %constant.135) | copy-start | bytes 786436
  33.9 158.8 %all-reduce.5.cloned.1.call-start = ((), (), s32[]{:S(2)}) async-start(), calls=%async_computation.1 | async-start | bytes 262144 | tf_op jit(solution)/shard_map/psum | solution.py:133
  110.4 1.9 copy-start.16
  113.9 2.7 %copy-start.4 = (f32[256,128]{1,0:T(8,128)S(1)}, f32[256,128]{1,0:T(8,128)}, u32[]{:S(2)}) copy-start(f32[256,128]{1,0:T(8,128)} %constant.133.clone) | copy-start | bytes 393220
  119.5 74.5 %copy-start.8 = (f32[640,128]{1,0:T(8,128)S(1)}, f32[640,128]{1,0:T(8,128)}, u32[]{:S(2)}) copy-start(f32[640,128]{1,0:T(8,128)} %constant.129.clone) | copy-start | bytes 983044
  194.4 2.6 %collective-permute-start.2 = (f32[64,128]{1,0:T(8,128)S(1)}, f32[64,128]{1,0:T(8,128)S(1)}, u32[]{:S(2)}, u32[]{:S(2)}) collective-permute-start(f32[64,128]{1,0:T(8,128)S(1)} %get-tuple-element.32), channel_id=1, source_target_pairs={{0,1},{2,3},{4,5},{6,7},{8,9},{10,11},{12,13},{14,15},{16,17},{18,... | collective-permute-start | bytes 98312 | tf_op jit(solution)/shard_map/ppermute | solution.py:137
  195.7 3.1 %collective-permute-start.3 = (f32[64,128]{1,0:T(8,128)S(1)}, f32[64,128]{1,0:T(8,128)S(1)}, u32[]{:S(2)}, u32[]{:S(2)}) collective-permute-start(f32[64,128]{1,0:T(8,128)S(1)} %get-tuple-element.31), channel_id=1, source_target_pairs={{1,0},{3,2},{5,4},{7,6},{9,8},{11,10},{13,12},{15,14},{17,16},{19,... | collective-permute-start | bytes 98312 | tf_op jit(solution)/shard_map/ppermute | solution.py:138
  197.0 1.8 copy-start.7
Sparse Core Ops, SparseCore 0:
  34.0 73.0 all-reduce.2
  123.2 69.4 all-reduce.4
where the time goes:
time: 208 us; the launch traced here: 207 us
  waiting for transfers between devices  142 us (68%)
  matrix products  27.2 us (13%)
  between operations  23.3 us (11%)
  starting transfers between devices  7.19 us (3%)
  other arithmetic  4.61 us (2%)
  local copies, waits for them, and re-layouts  2.58 us (1%)
    psum x1, waiting for transfers between devices, shards(): light = lax.psum(light, 'src')  70.7 us
    psum x1, waiting for transfers between devices, shards(): grid_grad = lax.psum(grid_grad, 'src')  69.6 us
    dot_general x41, matrix products, mm(): jnp.dot(a, b, precision=exact_mode, preferred_element_type=jnp.float32)  27.2 us
  transfers between devices with their start and end apart: 6, of which 3 were waited for; matrix products, arithmetic and copies ran while one was open for 3% of the time, Pallas kernels for 0%

commit v1 on v0

--- a/solution.py
+++ b/solution.py
@@ -104,7 +104,7 @@
         field = mm(turn, jnp.concatenate([real, imag], axis=0))
         fields.append(field)
         light = light + w * (field[:GRID] * field[:GRID] + field[GRID:] * field[GRID:])
-    light = lax.psum(light, "src")
+    light = jnp.sum(lax.all_gather(light, "src"), axis=0)
     up = mm(core, light)
     backs = []
     for c in range(tiles):

time: 208 us -> 178 us (0.86)
  waiting for transfers between devices: 142 us -> 111 us
    psum x1 -> x0, waiting for transfers between devices: 70.7 us -> none  [shards(): light = lax.psum(light, 'src')]
    all_gather x0 -> x1, waiting for transfers between devices: none -> 39.4 us  [shards(): light = jnp.sum(lax.all_gather(light, 'src'), axis=0)]
where the time goes in v1:
time: 178 us; the launch traced here: 177 us
  waiting for transfers between devices  111 us (62%)
  matrix products  26.6 us (15%)
  between operations  23.5 us (13%)
  starting transfers between devices  7.19 us (4%)
  other arithmetic  5.22 us (3%)
  local copies, waits for them, and re-layouts  4.01 us (2%)
    psum x1, waiting for transfers between devices, shards(): grid_grad = lax.psum(grid_grad, 'src')  69.6 us
    all_gather x1, waiting for transfers between devices, shards(): light = jnp.sum(lax.all_gather(light, 'src'), axis=0)  39.4 us
    dot_general x41, matrix products, mm(): jnp.dot(a, b, precision=exact_mode, preferred_element_type=jnp.float32)  26.6 us
  transfers between devices with their start and end apart: 6, of which 3 were waited for; matrix products, arithmetic and copies ran while one was open for 3% of the time, Pallas kernels for 0%

profile of v1, /device:TPU:0, one launch (start us, length us, event | category | flops | bytes accessed | tf_op | source)
XLA Modules:
  0.0 177.4 jit_solution(7165869082882650602)
XLA Ops:
  6.6 1.1 fusion.238
  7.7 1.3 collective-permute-start.1
  9.0 3.1 %collective-permute-start = (f32[64,1024]{1,0:T(8,128)S(1)}, f32[64,1024]{1,0:T(8,128)S(1)}, u32[]{:S(2)}, u32[]{:S(2)}) collective-permute-start(f32[64,1024]{1,0:T(8,128)S(1)} %get-tuple-element.29), channel_id=1, source_target_pairs={{0,1},{2,3},{4,5},{6,7},{8,9},{10,11},{12,13},{14,15},{16,17},{18,... | collective-permute-start | bytes 786440 | tf_op jit(solution)/shard_map/ppermute | solution.py:81
  12.0 3.0 %fusion.247 = f32[128,1024]{1,0:T(8,128)S(1)} fusion(f32[512,128]{1,0:T(8,128)} %constant.135, f32[512,1024]{1,0:T(8,128)} %param.14), kind=kOutput, calls=%fused_computation.328 | convolution fusion | flops 805306368 | bytes 2883584 | tf_op jit(solution)/shard_map/dot_general | solution.py:44
  15.1 0.7 constant_dynamic-slice_fusion.4
  23.1 0.7 fusion.246
  23.8 0.6 fusion.248
  24.5 0.7 fusion.10
  25.2 0.6 fusion.249
  26.5 0.4 convolution_multiply_fusion.4
  26.9 0.3 fusion.253
  27.3 0.4 convolution_multiply_fusion.3
  28.1 0.4 convolution_multiply_fusion.5
  28.9 0.4 fusion.161
  29.3 0.4 fusion.168
  29.7 0.4 fusion.154
  30.2 0.4 fusion.12
  30.6 0.4 fusion.11
  31.0 0.4 fusion.13
  31.5 2.7 %fusion.134 = f32[128,256]{0,1:T(8,128)} fusion(f32[256,256]{0,1:T(8,128)S(1)} %fusion.11, f32[256,256]{0,1:T(8,128)S(1)} %fusion.12, f32[256,256]{0,1:T(8,128)S(1)} %fusion.13, f32[]{:T(128)} %bitcast.17, f32[]{:T(128)} %bitcast.9, f32[]{:T(128)} %bitcast.8), kind=kLoop, calls=%fused_computation.153 | loop fusion | flops 458752 | bytes 917516 | tf_op jit(solution)/shard_map/add | solution.py:106
  36.3 0.7 reduce_sum.19
  37.0 39.4 %all-gather.3.cloned.1.call-done = f32[1024,256]{0,1:T(8,128)} async-done(((f32[128,256]{0,1:T(8,128)}), f32[1024,256]{0,1:T(8,128)}) %all-gather.3.cloned.1.call-update) | async-done | bytes 1048592 | tf_op jit(solution)/shard_map/all_gather | solution.py:107
  76.4 1.4 copy.16
  78.1 0.6 fusion.255
  78.7 1.8 %fusion.15 = f32[512,512]{1,0:T(8,128)S(1)} fusion(f32[512,128]{1,0:T(8,128)S(1)} %copy-done, f32[]{:T(128)} %reduce_sum.19, f32[512,256]{1,0:T(8,128)S(1)} %fusion.255), kind=kOutput, calls=%fused_computation.21 | convolution fusion | flops 404226048 | bytes 1572868 | tf_op jit(solution)/shard_map/dot_general | solution.py:44
  80.6 2.0 %fusion.14 = f32[512,512]{1,0:T(8,128)S(1)} fusion(f32[512,128]{1,0:T(8,128)S(1)} %copy-done, f32[]{:T(128)} %reduce_sum.19, f32[512,256]{1,0:T(8,128)S(1)} %fusion.255), kind=kOutput, calls=%fused_computation.20 | convolution fusion | flops 404226048 | bytes 1572868 | tf_op jit(solution)/shard_map/dot_general | solution.py:44
  82.5 1.7 fusion.16
  84.3 1.8 fusion.17
  86.0 1.0 fusion.18
  87.1 0.4 fusion.85
  87.5 0.4 convolution_multiply_fusion
  87.9 0.4 fusion.145
  88.2 0.4 fusion.82
  88.7 0.4 convolution_multiply_fusion.1
  89.0 0.4 fusion.148
  89.4 0.4 fusion.79
  89.9 0.4 convolution_multiply_fusion.2
  90.3 0.4 fusion.151
  91.0 0.4 convolution_subtract_fusion.2
  91.7 0.4 convolution_subtract_fusion.1
  92.4 1.1 convolution_subtract_fusion
  93.5 69.6 %all-reduce.2.cloned.1.call-done = f32[128,256]{1,0:T(8,128)} async-done(((f32[128,256]{1,0:T(8,128)}), f32[128,256]{1,0:T(8,128)}) %all-reduce.2.cloned.1.call-update) | async-done | bytes 131088 | tf_op jit(solution)/shard_map/psum | solution.py:133
  163.1 1.2 fusion.140
  164.3 0.4 fusion.256
  164.7 1.3 collective-permute-start.2
  166.1 1.3 collective-permute-start.3
  167.4 1.8 collective-permute-done.3
  169.2 1.4 fusion.194
  (70 shorter events, 3.1 us)
Async XLA Ops:
  6.5 17.3 %copy-start.12 = (f32[64,128]{1,0:T(8,128)S(1)}, f32[64,128]{1,0:T(8,128)}, u32[]{:S(2)}) copy-start(f32[64,128]{1,0:T(8,128)} %constant.136) | copy-start | bytes 98308
  6.5 8.5 %copy-start.13 = (f32[64,64]{1,0:T(8,128)S(1)}, f32[64,64]{1,0:T(8,128)}, u32[]{:S(2)}) copy-start(f32[64,64]{1,0:T(8,128)} %param.16) | copy-start | bytes 49156
  6.5 8.5 %copy-start.14 = (s32[24,2]{0,1:T(2,128)S(1)}, s32[24,2]{0,1:T(2,128)}, u32[]{:S(2)}) copy-start(s32[24,2]{0,1:T(2,128)} %param.17) | copy-start | bytes 580
  6.5 16.6 %copy-start.15 = (f32[24]{0:T(128)S(1)}, f32[24]{0:T(128)}, u32[]{:S(2)}) copy-start(f32[24]{0:T(128)} %param.18) | copy-start | bytes 292
  6.5 69.9 %all-gather.3.cloned.1.call-start = ((), (), s32[]{:S(2)}) async-start(), calls=%async_computation.1 | async-start | bytes 1179648 | tf_op jit(solution)/shard_map/all_gather | solution.py:107
  7.7 16.8 %copy-start.11 = (f32[64,128]{1,0:T(8,128)S(1)}, f32[64,128]{1,0:T(8,128)}, u32[]{:S(2)}) copy-start(f32[64,128]{1,0:T(8,128)} %constant.134) | copy-start | bytes 98308
  7.7 16.1 %collective-permute-start.1 = (f32[64,1024]{1,0:T(8,128)S(1)}, f32[64,1024]{1,0:T(8,128)S(1)}, u32[]{:S(2)}, u32[]{:S(2)}) collective-permute-start(f32[64,1024]{1,0:T(8,128)S(1)} %get-tuple-element.30), channel_id=1, source_target_pairs={{1,0},{3,2},{5,4},{7,6},{9,8},{11,10},{13,12},{15,14},{17,16},{19,... | collective-permute-start | bytes 786440 | tf_op jit(solution)/shard_map/ppermute | solution.py:82
  9.0 15.5 %collective-permute-start = (f32[64,1024]{1,0:T(8,128)S(1)}, f32[64,1024]{1,0:T(8,128)S(1)}, u32[]{:S(2)}, u32[]{:S(2)}) collective-permute-start(f32[64,1024]{1,0:T(8,128)S(1)} %get-tuple-element.29), channel_id=1, source_target_pairs={{0,1},{2,3},{4,5},{6,7},{8,9},{10,11},{12,13},{14,15},{16,17},{18,... | collective-permute-start | bytes 786440 | tf_op jit(solution)/shard_map/ppermute | solution.py:81
  15.0 10.1 %copy-start.2 = (f32[1024,256]{1,0:T(8,128)S(1)}, f32[1024,256]{1,0:T(8,128)}, u32[]{:S(2)}) copy-start(f32[1024,256]{1,0:T(8,128)} %constant.130.clone) | copy-start | bytes 3145732
  23.8 2.0 %copy-start.10 = (f32[112,128]{1,0:T(8,128)S(1)}, f32[112,128]{1,0:T(8,128)}, u32[]{:S(2)}) copy-start(f32[112,128]{1,0:T(8,128)} %constant.137) | copy-start | bytes 172036
  24.4 1.7 copy-start.9
  25.2 1.3 copy-start.1
  25.2 1.7 copy-start.6
  27.3 1.6 copy-start.3
  28.0 2.1 %copy-start.5 = (f32[256,64]{1,0:T(8,128)S(1)}, f32[256,64]{1,0:T(8,128)}, u32[]{:S(2)}) copy-start(f32[256,64]{1,0:T(8,128)} %constant.140) | copy-start | bytes 196612
  31.4 46.7 %copy-start = (f32[512,128]{1,0:T(8,128)S(1)}, f32[512,128]{1,0:T(8,128)}, u32[]{:S(2)}) copy-start(f32[512,128]{1,0:T(8,128)} %constant.135) | copy-start | bytes 786436
  34.2 128.9 %all-reduce.2.cloned.1.call-start = ((), (), s32[]{:S(2)}) async-start(), calls=%async_computation | async-start | bytes 262144 | tf_op jit(solution)/shard_map/psum | solution.py:133
  80.5 2.0 %copy-start.16 = (f32[512,1024]{1,0:T(8,128)S(1)}, f32[512,1024]{1,0:T(8,128)}, u32[]{:S(2)}) copy-start(f32[512,1024]{1,0:T(8,128)} %param.15) | copy-start | bytes 6291460
  84.3 2.8 %copy-start.4 = (f32[256,128]{1,0:T(8,128)S(1)}, f32[256,128]{1,0:T(8,128)}, u32[]{:S(2)}) copy-start(f32[256,128]{1,0:T(8,128)} %constant.133.clone) | copy-start | bytes 393220
  89.9 74.4 %copy-start.8 = (f32[640,128]{1,0:T(8,128)S(1)}, f32[640,128]{1,0:T(8,128)}, u32[]{:S(2)}) copy-start(f32[640,128]{1,0:T(8,128)} %constant.129.clone) | copy-start | bytes 983044
  164.7 2.6 %collective-permute-start.2 = (f32[64,128]{1,0:T(8,128)S(1)}, f32[64,128]{1,0:T(8,128)S(1)}, u32[]{:S(2)}, u32[]{:S(2)}) collective-permute-start(f32[64,128]{1,0:T(8,128)S(1)} %get-tuple-element.32), channel_id=1, source_target_pairs={{0,1},{2,3},{4,5},{6,7},{8,9},{10,11},{12,13},{14,15},{16,17},{18,... | collective-permute-start | bytes 98312 | tf_op jit(solution)/shard_map/ppermute | solution.py:137
  166.1 3.1 %collective-permute-start.3 = (f32[64,128]{1,0:T(8,128)S(1)}, f32[64,128]{1,0:T(8,128)S(1)}, u32[]{:S(2)}, u32[]{:S(2)}) collective-permute-start(f32[64,128]{1,0:T(8,128)S(1)} %get-tuple-element.31), channel_id=1, source_target_pairs={{1,0},{3,2},{5,4},{7,6},{9,8},{11,10},{13,12},{15,14},{17,16},{19,... | collective-permute-start | bytes 98312 | tf_op jit(solution)/shard_map/ppermute | solution.py:138
  167.4 1.8 %copy-start.7 = (f32[512,128]{1,0:T(8,128)}, f32[512,128]{1,0:T(8,128)S(1)}, u32[]{:S(2)}) copy-start(f32[512,128]{1,0:T(8,128)S(1)} %fusion.195) | copy-start | bytes 786436
Sparse Core Ops, SparseCore 0:
  34.3 42.0 all-gather.2
  93.6 69.4 all-reduce.1
